TPU v7x, 32 devices: a whole 2x2x4 slice. The times are simulated.
32 devices in a mesh: seq: 8 (over z, x), tp: 4 (over y, core).
Axes of the slice: x: 2, y: 2, z: 4, core: 2. Of those that a mesh axis runs over, the one named last changes fastest.
Arguments:
- hidden_in: bfloat16 [16, 2048], replicated, may hold values from -6 to 6
- lengths: int32 [16], replicated, may hold values from 1 to 511, 2431 in all
- positions: int32 [16], replicated, may hold values from 0 to 1023
- query_weight: bfloat16 [2, 2048, 2048], P(None, 'seq', 'tp'), may hold values from -0.125 to 0.125
- key_weight: bfloat16 [2, 2048, 512], P(None, 'seq', 'tp'), may hold values from -4 to 4
- value_weight: bfloat16 [2, 2048, 512], P(None, 'seq', 'tp'), may hold values from -0.125 to 0.125
- out_weight: bfloat16 [2, 2048, 2048], P(None, 'tp', 'seq'), may hold values from -0.125 to 0.125
- gate_weight: bfloat16 [2, 2048, 8192], P(None, 'seq', 'tp'), may hold values from -0.125 to 0.125
- up_weight: bfloat16 [2, 2048, 8192], P(None, 'seq', 'tp'), may hold values from -0.125 to 0.125
- down_weight: bfloat16 [2, 8192, 2048], P(None, 'tp', 'seq'), may hold values from -0.0625 to 0.0625
- key_cache: bfloat16 [2, 16, 512, 512], P(None, None, 'seq', 'tp'), may hold values from -80 to 80
- value_cache: bfloat16 [2, 16, 512, 512], P(None, None, 'seq', 'tp'), may hold values from -6 to 6
Outputs:
- hidden_out: bfloat16 [16, 2048], replicated
- key_out: bfloat16 [2, 16, 512, 512], P(None, None, 'seq', 'tp')
- value_out: bfloat16 [2, 16, 512, 512], P(None, None, 'seq', 'tp')
Inputs may be any that keep to these rules, and one draw needn't show every extreme that they name: Request b has its cached rows at positions 0 .. lengths[b] - 1 and its new token goes to row lengths[b]; rows above are padding. The longest request has exactly 511 cached rows.
All inputs are finite; a program needn't handle non-finite values.
Results may differ from a plain program's by a relative error of at most 0.015.
Values may be sent and summed in bfloat16 or wider, within the bound.
No kernel may reach another device: no remote copies, remote signals or barrier semaphores. Data moves between devices by JAX's collectives and lax.ppermute only.
A program may use at most 64 MiB of HBM per device.

v0:
```python
import math
import jax
import jax.numpy as jnp
from jax import lax
from jax.sharding import PartitionSpec as P

HEAD_DIM = 64
LAYERS = 2
eps_norm = 1e-05
neg_fill = -1e30


def rms_norm(stream):
    as_float = stream.astype(jnp.float32)
    spread = jnp.mean(as_float * as_float, axis=-1, keepdims=True)
    return (as_float * lax.rsqrt(spread + eps_norm)).astype(jnp.bfloat16)


def rotate(heads, positions):
    half_dim = heads.shape[-1] // 2
    inverse = 500000.0 ** (-(2.0 * jnp.arange(half_dim, dtype=jnp.float32)) / heads.shape[-1])
    angles = positions.astype(jnp.float32)[:, None] * inverse[None, :]
    cosine = jnp.cos(angles)[:, None, :]
    sine = jnp.sin(angles)[:, None, :]
    first_half = heads[..., :half_dim]
    second_half = heads[..., half_dim:]
    return jnp.concatenate(
        [first_half * cosine - second_half * sine, second_half * cosine + first_half * sine],
        axis=-1,
    )


def per_device(
    hidden_in,
    lengths,
    positions,
    query_weight,
    key_weight,
    value_weight,
    out_weight,
    gate_weight,
    up_weight,
    down_weight,
    key_cache,
    value_cache,
):
    seq_index = lax.axis_index("seq")
    row_count = query_weight.shape[1]
    row_start = seq_index * row_count
    col_count = out_weight.shape[2]
    col_start = seq_index * col_count
    block_len = key_cache.shape[2]
    kv_width_here = key_cache.shape[3]
    query_width = query_weight.shape[2]
    requests = hidden_in.shape[0]
    group_heads = query_width // HEAD_DIM
    kv_here = kv_width_here // HEAD_DIM
    repeat = group_heads // kv_here
    score_scale = 1.0 / math.sqrt(HEAD_DIM)
    global_slots = seq_index * block_len + jnp.arange(block_len, dtype=jnp.int32)
    new_slot = (global_slots[None, :] == lengths[:, None])[:, :, None]
    live_mask = (global_slots[None, :] <= lengths[:, None])[:, None, None, :]

    def finish(part_terms, stream_now):
        summed = lax.psum(part_terms, "tp")
        own_cols = lax.dynamic_slice_in_dim(stream_now, col_start, col_count, 1).astype(jnp.float32)
        return lax.all_gather((own_cols + summed).astype(jnp.bfloat16), "seq", axis=1, tiled=True)

    stream = hidden_in
    key_layers = []
    value_layers = []
    for layer_idx in range(LAYERS):
        normed = rms_norm(stream)
        own_rows = lax.dynamic_slice_in_dim(normed, row_start, row_count, 1)
        query_part = jnp.dot(own_rows, query_weight[layer_idx], preferred_element_type=jnp.float32)
        key_part = jnp.dot(own_rows, key_weight[layer_idx], preferred_element_type=jnp.float32)
        value_part = jnp.dot(own_rows, value_weight[layer_idx], preferred_element_type=jnp.float32)
        query, key_new, value_new = lax.psum((query_part, key_part, value_part), "seq")
        query = rotate(query.reshape(requests, group_heads, HEAD_DIM), positions).astype(
            jnp.bfloat16
        )
        query = query.reshape(requests, kv_here, repeat, HEAD_DIM)
        key_new = (
            rotate(key_new.reshape(requests, kv_here, HEAD_DIM), positions)
            .astype(jnp.bfloat16)
            .reshape(requests, kv_width_here)
        )
        value_new = value_new.astype(jnp.bfloat16)
        key_rows = jnp.where(new_slot, key_new[:, None, :], key_cache[layer_idx])
        value_rows = jnp.where(new_slot, value_new[:, None, :], value_cache[layer_idx])
        key_heads = key_rows.reshape(requests, block_len, kv_here, HEAD_DIM)
        value_heads = value_rows.reshape(requests, block_len, kv_here, HEAD_DIM)
        scores = (
            jnp.einsum("bkrd,bskd->bkrs", query, key_heads, preferred_element_type=jnp.float32)
            * score_scale
        )
        scores = jnp.where(live_mask, scores, neg_fill)
        row_top = lax.pmax(jnp.max(scores, axis=3), "seq")
        weights = jnp.where(live_mask, jnp.exp(scores - row_top[..., None]), 0.0)
        local_sums = jnp.sum(weights, axis=3)
        local_acc = jnp.einsum(
            "bkrs,bskd->bkrd",
            weights.astype(jnp.bfloat16),
            value_heads,
            preferred_element_type=jnp.float32,
        )
        totals, weighted = lax.psum((local_sums, local_acc), "seq")
        attended = (
            (weighted / totals[..., None]).astype(jnp.bfloat16).reshape(requests, query_width)
        )
        attn_terms = jnp.dot(attended, out_weight[layer_idx], preferred_element_type=jnp.float32)
        mid = finish(attn_terms, stream)
        normed_two = rms_norm(mid)
        rows_two = lax.dynamic_slice_in_dim(normed_two, row_start, row_count, 1)
        gate_part = jnp.dot(rows_two, gate_weight[layer_idx], preferred_element_type=jnp.float32)
        up_part = jnp.dot(rows_two, up_weight[layer_idx], preferred_element_type=jnp.float32)
        gate_sum, up_sum = lax.psum((gate_part, up_part), "seq")
        hidden = (jax.nn.silu(gate_sum) * up_sum).astype(jnp.bfloat16)
        down_terms = jnp.dot(hidden, down_weight[layer_idx], preferred_element_type=jnp.float32)
        stream = finish(down_terms, mid)
        key_layers.append(key_rows)
        value_layers.append(value_rows)
    return (stream, jnp.stack(key_layers), jnp.stack(value_layers))


def solution(mesh):
    return jax.shard_map(
        per_device,
        mesh=mesh,
        in_specs=(
            P(),
            P(),
            P(),
            P(None, "seq", "tp"),
            P(None, "seq", "tp"),
            P(None, "seq", "tp"),
            P(None, "tp", "seq"),
            P(None, "seq", "tp"),
            P(None, "seq", "tp"),
            P(None, "tp", "seq"),
            P(None, None, "seq", "tp"),
            P(None, None, "seq", "tp"),
        ),
        out_specs=(P(), P(None, None, "seq", "tp"), P(None, None, "seq", "tp")),
        check_vma=False,
    )
```

profile of v0, /device:TPU:0, one launch (start us, length us, event | category | flops | bytes accessed | tf_op | source)
XLA Modules:
  0.0 562.6 jit_solution(6855281874656980006)
XLA Ops:
  13.7 39.8 %all-reduce.3 = (bf16[16,128]{1,0:T(8,128)(2,1)S(1)}, f32[16,2,64]{2,1,0:T(2,128)S(1)}, f32[16,8,64]{2,1,0:T(8,128)S(1)}) all-reduce(f32[16,128]{1,0:T(8,128)S(1)} %fusion.46, f32[16,2,64]{2,1,0:T(2,128)S(1)} %reshape.206, f32[16,8,64]{2,1,0:T(8,128)S(1)} %reshape.205), channel_id=1, replica_groups=mesh['seq'=8,'tp'=4] {'seq'}, use_global_device_ids=true, to_apply=%region_5.6 | all-reduce | flops 12288 | bytes 94208 | tf_op jit(solution)/shard_map/psum | solution.py:78
  55.8 1.7 fusion.88
  57.5 33.0 %pmax.14 = f32[16,2,4]{2,1,0:T(2,128)S(1)} all-reduce(f32[16,2,4]{2,1,0:T(2,128)S(1)} %get-tuple-element.38), channel_id=1, replica_groups=mesh['seq'=8,'tp'=4] {'seq'}, use_global_device_ids=true, to_apply=%region_4.5 | all-reduce | flops 128 | bytes 1024 | tf_op jit(solution)/shard_map/pmax | solution.py:98
  91.8 33.8 %all-reduce.2 = (f32[16,2,4,64]{3,2,1,0:T(4,128)S(1)}, f32[16,2,4]{2,1,0:T(2,128)S(1)}) all-reduce(f32[16,2,4,64]{3,2,1,0:T(4,128)S(1)} %fusion.21, f32[16,2,4]{2,1,0:T(2,128)S(1)} %fusion.56), channel_id=1, replica_groups=mesh['seq'=8,'tp'=4] {'seq'}, use_global_device_ids=true, to_apply=%region_6.7 | all-reduce | flops 8320 | bytes 66560 | tf_op jit(solution)/shard_map/psum | solution.py:107
  126.0 10.1 %psum.131 = f32[16,256]{1,0:T(8,128)S(1)} all-reduce(f32[16,256]{1,0:T(8,128)S(1)} %fusion.30), channel_id=1, replica_groups=mesh['seq'=8,'tp'=4] {'tp'}, use_global_device_ids=true, to_apply=%region_9.10 | all-reduce | flops 4096 | bytes 32768 | tf_op jit(solution)/shard_map/psum | solution.py:65
  136.8 30.5 %all_gather.12 = bf16[16,2048]{1,0:T(8,128)(2,1)S(1)} all-gather(bf16[16,256]{1,0:T(8,128)(2,1)S(1)} %add_convert_fusion.5), channel_id=1, replica_groups=mesh['seq'=8,'tp'=4] {'seq'}, dimensions={1}, use_global_device_ids=true | all-gather | bytes 73728 | tf_op jit(solution)/shard_map/all_gather | solution.py:67
  168.4 2.3 fusion.12
  171.4 69.2 %all-reduce.11.cloned.1.call-done = (f32[16,2048]{1,0:T(8,128)}, f32[16,2048]{1,0:T(8,128)}) async-done(((f32[16,2048]{1,0:T(8,128)}, f32[16,2048]{1,0:T(8,128)}), (f32[16,2048]{1,0:T(8,128)}, f32[16,2048]{1,0:T(8,128)})) %all-reduce.11.cloned.1.call-update) | async-done | bytes 262160 | tf_op jit(solution)/shard_map/psum | solution.py:117
  240.6 1.6 fusion.8
  242.2 10.1 %psum.134 = f32[16,256]{1,0:T(8,128)S(1)} all-reduce(f32[16,256]{1,0:T(8,128)S(1)} %fusion.8), channel_id=1, replica_groups=mesh['seq'=8,'tp'=4] {'tp'}, use_global_device_ids=true, to_apply=%region_13.14 | all-reduce | flops 4096 | bytes 32768 | tf_op jit(solution)/shard_map/psum | solution.py:65
  252.3 30.5 %all_gather.13 = bf16[16,2048]{1,0:T(8,128)(2,1)S(1)} all-gather(bf16[16,256]{1,0:T(8,128)(2,1)S(1)} %add_convert_fusion.4), channel_id=1, replica_groups=mesh['seq'=8,'tp'=4] {'seq'}, dimensions={1}, use_global_device_ids=true | all-gather | bytes 73728 | tf_op jit(solution)/shard_map/all_gather | solution.py:67
  286.4 36.4 %all-reduce.1 = (bf16[16,128]{1,0:T(8,128)(2,1)S(1)}, f32[16,2,64]{2,1,0:T(2,128)S(1)}, f32[16,8,64]{2,1,0:T(8,128)S(1)}) all-reduce(f32[16,128]{1,0:T(8,128)S(1)} %fusion.42, f32[16,2,64]{2,1,0:T(2,128)S(1)} %reshape.209, f32[16,8,64]{2,1,0:T(8,128)S(1)} %reshape.208), channel_id=1, replica_groups=mesh['seq'=8,'tp'=4] {'seq'}, use_global_device_ids=true, to_apply=%region_19.20 | all-reduce | flops 12288 | bytes 94208 | tf_op jit(solution)/shard_map/psum | solution.py:78
  324.4 1.9 broadcast_select_fusion.1
  326.2 1.2 squeeze.67
  327.8 1.2 fusion.89
  329.0 33.0 %pmax.15 = f32[16,2,4]{2,1,0:T(2,128)S(1)} all-reduce(f32[16,2,4]{2,1,0:T(2,128)S(1)} %get-tuple-element.40), channel_id=1, replica_groups=mesh['seq'=8,'tp'=4] {'seq'}, use_global_device_ids=true, to_apply=%region_18.19 | all-reduce | flops 128 | bytes 1024 | tf_op jit(solution)/shard_map/pmax | solution.py:98
  364.0 34.0 %all-reduce = (f32[16,2,4,64]{3,2,1,0:T(4,128)S(1)}, f32[16,2,4]{2,1,0:T(2,128)S(1)}) all-reduce(f32[16,2,4,64]{3,2,1,0:T(4,128)S(1)} %fusion.20, f32[16,2,4]{2,1,0:T(2,128)S(1)} %fusion.58), channel_id=1, replica_groups=mesh['seq'=8,'tp'=4] {'seq'}, use_global_device_ids=true, to_apply=%region_20.21 | all-reduce | flops 8320 | bytes 66560 | tf_op jit(solution)/shard_map/psum | solution.py:107
  399.3 10.1 %psum.140 = f32[16,256]{1,0:T(8,128)S(1)} all-reduce(f32[16,256]{1,0:T(8,128)S(1)} %fusion.26), channel_id=1, replica_groups=mesh['seq'=8,'tp'=4] {'tp'}, use_global_device_ids=true, to_apply=%region_23.24 | all-reduce | flops 4096 | bytes 32768 | tf_op jit(solution)/shard_map/psum | solution.py:65
  409.4 30.5 %all_gather.14 = bf16[16,2048]{1,0:T(8,128)(2,1)S(1)} all-gather(bf16[16,256]{1,0:T(8,128)(2,1)S(1)} %add_convert_fusion.3), channel_id=1, replica_groups=mesh['seq'=8,'tp'=4] {'seq'}, dimensions={1}, use_global_device_ids=true | all-gather | bytes 73728 | tf_op jit(solution)/shard_map/all_gather | solution.py:67
  441.0 2.3 fusion.6
  444.4 68.8 %all-reduce.9.cloned.1.call-done = (f32[16,2048]{1,0:T(8,128)}, f32[16,2048]{1,0:T(8,128)}) async-done(((f32[16,2048]{1,0:T(8,128)}, f32[16,2048]{1,0:T(8,128)}), (f32[16,2048]{1,0:T(8,128)}, f32[16,2048]{1,0:T(8,128)})) %all-reduce.9.cloned.1.call-update) | async-done | bytes 262160 | tf_op jit(solution)/shard_map/psum | solution.py:117
  513.3 1.2 fusion.2
  514.5 10.1 %psum.143 = f32[16,256]{1,0:T(8,128)S(1)} all-reduce(f32[16,256]{1,0:T(8,128)S(1)} %fusion.2), channel_id=1, replica_groups=mesh['seq'=8,'tp'=4] {'tp'}, use_global_device_ids=true, to_apply=%region_27.28 | all-reduce | flops 4096 | bytes 32768 | tf_op jit(solution)/shard_map/psum | solution.py:65
  524.6 30.5 %all_gather.15 = bf16[16,2048]{1,0:T(8,128)(2,1)S(1)} all-gather(bf16[16,256]{1,0:T(8,128)(2,1)S(1)} %add_convert_fusion.2), channel_id=1, replica_groups=mesh['seq'=8,'tp'=4] {'seq'}, dimensions={1}, use_global_device_ids=true | all-gather | bytes 73728 | tf_op jit(solution)/shard_map/all_gather | solution.py:67
  (97 shorter events, 24.3 us)
Async XLA Ops:
  7.2 47.1 %slice-start = ((bf16[2,16,64,128]{3,2,1,0:T(8,128)(2,1)}), bf16[1,16,64,128]{3,2,1,0:T(8,128)(2,1)S(1)}, s32[]{:S(2)}) async-start(bf16[2,16,64,128]{3,2,1,0:T(8,128)(2,1)} %param.22), calls=%async_computation.2 | async-start | bytes 524288 | tf_op jit(solution)/shard_map/slice | solution.py:89
  7.2 48.1 %copy-start.15 = (s32[16]{0:T(128)S(1)}, s32[16]{0:T(128)}, u32[]{:S(2)}) copy-start(s32[16]{0:T(128)} %param.14) | copy-start | bytes 196
  7.2 48.5 %copy-start.13 = (s32[16]{0:T(128)S(1)}, s32[16]{0:T(128)}, u32[]{:S(2)}) copy-start(s32[16]{0:T(128)} %param.13) | copy-start | bytes 196
  7.2 233.4 %all-reduce.11.cloned.1.call-start = ((), (), s32[]{:S(2)}) async-start(), calls=%async_computation.1 | async-start | bytes 524288 | tf_op jit(solution)/shard_map/psum | solution.py:117
  53.6 0.7 copy-start.10
  54.3 71.6 %copy-start.7 = (bf16[2,512,256]{2,1,0:T(8,128)(2,1)S(1)}, bf16[2,512,256]{2,1,0:T(8,128)(2,1)}, u32[]{:S(2)}) copy-start(bf16[2,512,256]{2,1,0:T(8,128)(2,1)} %param.18) | copy-start | bytes 1572868
  55.5 111.9 %copy-start = (bf16[2,256,2048]{2,1,0:T(8,128)(2,1)S(1)}, bf16[2,256,2048]{2,1,0:T(8,128)(2,1)}, u32[]{:S(2)}) copy-start(bf16[2,256,2048]{2,1,0:T(8,128)(2,1)} %param.20) | copy-start | bytes 6291460
  55.7 112.7 %copy-start.9 = (pred[16,64]{1,0:T(8,128)(4,1)}, pred[16,64]{1,0:T(8,128)(4,1)S(1)}, u32[]{:S(2)}) copy-start(pred[16,64]{1,0:T(8,128)(4,1)S(1)} %get-tuple-element.34) | copy-start | bytes 3076
  55.7 112.7 %copy-start.12 = (pred[16,64]{1,0:T(8,128)(4,1)}, pred[16,64]{1,0:T(8,128)(4,1)S(1)}, u32[]{:S(2)}) copy-start(pred[16,64]{1,0:T(8,128)(4,1)S(1)} %get-tuple-element.35) | copy-start | bytes 3076
  168.4 155.9 %copy-start.1 = (bf16[2,16,64,128]{3,2,1,0:T(8,128)(2,1)S(1)}, bf16[2,16,64,128]{3,2,1,0:T(8,128)(2,1)}, u32[]{:S(2)}) copy-start(bf16[2,16,64,128]{3,2,1,0:T(8,128)(2,1)} %param.23) | copy-start | bytes 1572868
  168.4 155.9 %copy-start.2 = (bf16[2,16,64,128]{3,2,1,0:T(8,128)(2,1)S(1)}, bf16[2,16,64,128]{3,2,1,0:T(8,128)(2,1)}, u32[]{:S(2)}) copy-start(bf16[2,16,64,128]{3,2,1,0:T(8,128)(2,1)} %param.22) | copy-start | bytes 1572868
  170.7 342.6 %all-reduce.9.cloned.1.call-start = ((), (), s32[]{:S(2)}) async-start(), calls=%async_computation | async-start | bytes 524288 | tf_op jit(solution)/shard_map/psum | solution.py:117
  322.8 0.9 copy-start.11
  323.0 0.7 copy-start.8
  364.0 79.4 %copy-start.3 = (bf16[1,16,64,128]{3,2,1,0:T(8,128)(2,1)S(1)}, bf16[1,16,64,128]{3,2,1,0:T(8,128)(2,1)}, u32[]{:S(2)}) copy-start(bf16[1,16,64,128]{3,2,1,0:T(8,128)(2,1)} %get-tuple-element.17) | copy-start | bytes 786436
  364.0 79.4 %copy-start.4 = (bf16[1,16,64,128]{3,2,1,0:T(8,128)(2,1)S(1)}, bf16[1,16,64,128]{3,2,1,0:T(8,128)(2,1)}, u32[]{:S(2)}) copy-start(bf16[1,16,64,128]{3,2,1,0:T(8,128)(2,1)} %get-tuple-element.18) | copy-start | bytes 786436
  364.0 79.4 %copy-start.5 = (bf16[1,16,64,128]{3,2,1,0:T(8,128)(2,1)S(1)}, bf16[1,16,64,128]{3,2,1,0:T(8,128)(2,1)}, u32[]{:S(2)}) copy-start(bf16[1,16,64,128]{3,2,1,0:T(8,128)(2,1)} %get-tuple-element.32) | copy-start | bytes 786436
  364.0 79.4 %copy-start.6 = (bf16[1,16,64,128]{3,2,1,0:T(8,128)(2,1)S(1)}, bf16[1,16,64,128]{3,2,1,0:T(8,128)(2,1)}, u32[]{:S(2)}) copy-start(bf16[1,16,64,128]{3,2,1,0:T(8,128)(2,1)} %get-tuple-element.33) | copy-start | bytes 786436
  441.0 72.3 %copy-start.14 = (bf16[2,2048,256]{2,1,0:T(8,128)(2,1)S(1)}, bf16[2,2048,256]{2,1,0:T(8,128)(2,1)}, u32[]{:S(2)}) copy-start(bf16[2,2048,256]{2,1,0:T(8,128)(2,1)} %param.21) | copy-start | bytes 6291460
Sparse Core Ops, SparseCore 0:
  170.8 69.7 all-reduce.10
  443.5 69.7 all-reduce.8
where the time goes:
time: 564 us; the launch traced here: 563 us
  blocking collectives  372 us (66%)
  waiting for transfers between devices  138 us (24%)
  matrix products  22 us (4%)
  between operations  14.4 us (3%)
  other arithmetic  8.02 us (1%)
  local copies, waits for them, and re-layouts  7.62 us (1%)
    psum x2, waiting for transfers between devices, per_device(): gate_sum, up_sum = lax.psum((gate_part, up_part), 'seq')  138 us
    all_gather x4, blocking collectives, finish(): lax.all_gather((own_cols + summed).astype(jnp.bfloat16), 'seq', axis=1, t...  122 us
    psum x2, blocking collectives, per_device(): lax.psum((query_part, key_part, value_part), 'seq')  76.3 us
    psum x2, blocking collectives, per_device(): totals, weighted = lax.psum((local_sums, local_acc), 'seq')  67.8 us
    pmax x2, blocking collectives, per_device(): row_top = lax.pmax(jnp.max(scores, axis=3), 'seq')  66 us
    psum x4, blocking collectives, finish(): summed = lax.psum(part_terms, 'tp')  40.5 us
  transfers between devices with their start and end apart: 2, of which 2 were waited for; matrix products, arithmetic and copies ran while one was open for 0% of the time, Pallas kernels for 0%

commit v1 on v0

--- a/solution.py
+++ b/solution.py
@@ -8,6 +8,18 @@
 LAYERS = 2
 eps_norm = 1e-05
 neg_fill = -1e30
+
+
+def doubled_up(shard, axis, dim):
+    ways, here = (lax.axis_size(axis), lax.axis_index(axis))
+    grown, reach = (shard, 1)
+    while reach < ways:
+        theirs = lax.ppermute(grown, axis, [(d, d ^ reach) for d in range(ways)])
+        mine_first = jnp.concatenate([grown, theirs], axis=dim)
+        theirs_first = jnp.concatenate([theirs, grown], axis=dim)
+        grown = jnp.where(here & reach == 0, mine_first, theirs_first)
+        reach = 2 * reach
+    return grown
 
 
 def rms_norm(stream):
@@ -64,7 +76,7 @@
     def finish(part_terms, stream_now):
         summed = lax.psum(part_terms, "tp")
         own_cols = lax.dynamic_slice_in_dim(stream_now, col_start, col_count, 1).astype(jnp.float32)
-        return lax.all_gather((own_cols + summed).astype(jnp.bfloat16), "seq", axis=1, tiled=True)
+        return doubled_up((own_cols + summed).astype(jnp.bfloat16), "seq", 1)
 
     stream = hidden_in
     key_layers = []

time: 564 us -> 492 us (0.87)
  blocking collectives: 372 us -> 250 us
  waiting for transfers between devices: 138 us -> 180 us
  starting transfers between devices: 0.08 us -> 7.82 us
    all_gather x4 -> x0, blocking collectives: 122 us -> none  [finish(): lax.all_gather((own_cols + summed).astype(jnp.bfloat16), 'seq', axis=1, t...]
    ppermute x0 -> x12, waiting for transfers between devices: none -> 39.7 us  [doubled_up(): theirs = lax.ppermute(grown, axis, [(d, d ^ reach) for d in range(ways)])]
    ppermute x0 -> x12, starting transfers between devices: none -> 7.74 us  [doubled_up(): theirs = lax.ppermute(grown, axis, [(d, d ^ reach) for d in range(ways)])]
  transfers between devices with their start and end apart: 2 -> 14, of which waited for: 2 -> 14; matrix products, arithmetic and copies ran while one was open for 0% -> 0% of each run, Pallas kernels for 0% -> 0%
where the time goes in v1:
time: 492 us; the launch traced here: 491 us
  blocking collectives  250 us (51%)
  waiting for transfers between devices  180 us (37%)
  matrix products  21.6 us (4%)
  between operations  14.5 us (3%)
  other arithmetic  8.73 us (2%)
  starting transfers between devices  7.82 us (2%)
  local copies, waits for them, and re-layouts  7.79 us (2%)
    psum x2, waiting for transfers between devices, per_device(): gate_sum, up_sum = lax.psum((gate_part, up_part), 'seq')  140 us
    psum x2, blocking collectives, per_device(): lax.psum((query_part, key_part, value_part), 'seq')  76.3 us
    psum x2, blocking collectives, per_device(): totals, weighted = lax.psum((local_sums, local_acc), 'seq')  67.7 us
    pmax x2, blocking collectives, per_device(): row_top = lax.pmax(jnp.max(scores, axis=3), 'seq')  66 us
    psum x4, blocking collectives, finish(): summed = lax.psum(part_terms, 'tp')  40.5 us
    ppermute x12, waiting for transfers between devices, doubled_up(): theirs = lax.ppermute(grown, axis, [(d, d ^ reach) for d in range(ways)])  39.7 us
  transfers between devices with their start and end apart: 14, of which 14 were waited for; matrix products, arithmetic and copies ran while one was open for 0% of the time, Pallas kernels for 0%

profile of v1, /device:TPU:0, one launch (start us, length us, event | category | flops | bytes accessed | tf_op | source)
XLA Modules:
  0.0 490.6 jit_solution(9308082766792576374)
XLA Ops:
  13.7 39.8 %all-reduce.3 = (bf16[16,128]{1,0:T(8,128)(2,1)S(1)}, f32[16,2,64]{2,1,0:T(2,128)S(1)}, f32[16,8,64]{2,1,0:T(8,128)S(1)}) all-reduce(f32[16,128]{1,0:T(8,128)S(1)} %fusion.46, f32[16,2,64]{2,1,0:T(2,128)S(1)} %reshape.206, f32[16,8,64]{2,1,0:T(8,128)S(1)} %reshape.205), channel_id=1, replica_groups=mesh['seq'=8,'tp'=4] {'seq'}, use_global_device_ids=true, to_apply=%region_5.6 | all-reduce | flops 12288 | bytes 94208 | tf_op jit(solution)/shard_map/psum | solution.py:90
  57.5 33.0 %pmax.14 = f32[16,2,4]{2,1,0:T(2,128)S(1)} all-reduce(f32[16,2,4]{2,1,0:T(2,128)S(1)} %get-tuple-element.44), channel_id=1, replica_groups=mesh['seq'=8,'tp'=4] {'seq'}, use_global_device_ids=true, to_apply=%region_4.5 | all-reduce | flops 128 | bytes 1024 | tf_op jit(solution)/shard_map/pmax | solution.py:110
  91.8 33.8 %all-reduce.2 = (f32[16,2,4,64]{3,2,1,0:T(4,128)S(1)}, f32[16,2,4]{2,1,0:T(2,128)S(1)}) all-reduce(f32[16,2,4,64]{3,2,1,0:T(4,128)S(1)} %fusion.21, f32[16,2,4]{2,1,0:T(2,128)S(1)} %fusion.56), channel_id=1, replica_groups=mesh['seq'=8,'tp'=4] {'seq'}, use_global_device_ids=true, to_apply=%region_6.7 | all-reduce | flops 8320 | bytes 66560 | tf_op jit(solution)/shard_map/psum | solution.py:119
  126.0 10.1 %psum.131 = f32[16,256]{1,0:T(8,128)S(1)} all-reduce(f32[16,256]{1,0:T(8,128)S(1)} %fusion.30), channel_id=1, replica_groups=mesh['seq'=8,'tp'=4] {'tp'}, use_global_device_ids=true, to_apply=%region_9.10 | all-reduce | flops 4096 | bytes 32768 | tf_op jit(solution)/shard_map/psum | solution.py:77
  136.8 3.6 collective-permute-done
  140.5 3.7 collective-permute-done.1
  144.3 4.8 collective-permute-done.2
  150.2 2.3 fusion.12
  152.6 70.0 %all-reduce.11.cloned.1.call-done = (f32[16,2048]{1,0:T(8,128)}, f32[16,2048]{1,0:T(8,128)}) async-done(((f32[16,2048]{1,0:T(8,128)}, f32[16,2048]{1,0:T(8,128)}), (f32[16,2048]{1,0:T(8,128)}, f32[16,2048]{1,0:T(8,128)})) %all-reduce.11.cloned.1.call-update) | async-done | bytes 262160 | tf_op jit(solution)/shard_map/psum | solution.py:129
  224.2 10.1 %psum.134 = f32[16,256]{1,0:T(8,128)S(1)} all-reduce(f32[16,256]{1,0:T(8,128)S(1)} %fusion.8), channel_id=1, replica_groups=mesh['seq'=8,'tp'=4] {'tp'}, use_global_device_ids=true, to_apply=%region_13.14 | all-reduce | flops 4096 | bytes 32768 | tf_op jit(solution)/shard_map/psum | solution.py:77
  235.1 2.9 collective-permute-done.3
  239.0 2.7 collective-permute-done.4
  244.3 2.3 collective-permute-done.5
  250.2 36.4 %all-reduce.1 = (bf16[16,128]{1,0:T(8,128)(2,1)S(1)}, f32[16,2,64]{2,1,0:T(2,128)S(1)}, f32[16,8,64]{2,1,0:T(8,128)S(1)}) all-reduce(f32[16,128]{1,0:T(8,128)S(1)} %fusion.42, f32[16,2,64]{2,1,0:T(2,128)S(1)} %reshape.209, f32[16,8,64]{2,1,0:T(8,128)S(1)} %reshape.208), channel_id=1, replica_groups=mesh['seq'=8,'tp'=4] {'seq'}, use_global_device_ids=true, to_apply=%region_19.20 | all-reduce | flops 12288 | bytes 94208 | tf_op jit(solution)/shard_map/psum | solution.py:90
  294.0 33.0 %pmax.15 = f32[16,2,4]{2,1,0:T(2,128)S(1)} all-reduce(f32[16,2,4]{2,1,0:T(2,128)S(1)} %get-tuple-element.46), channel_id=1, replica_groups=mesh['seq'=8,'tp'=4] {'seq'}, use_global_device_ids=true, to_apply=%region_18.19 | all-reduce | flops 128 | bytes 1024 | tf_op jit(solution)/shard_map/pmax | solution.py:110
  328.9 33.9 %all-reduce = (f32[16,2,4,64]{3,2,1,0:T(4,128)S(1)}, f32[16,2,4]{2,1,0:T(2,128)S(1)}) all-reduce(f32[16,2,4,64]{3,2,1,0:T(4,128)S(1)} %fusion.20, f32[16,2,4]{2,1,0:T(2,128)S(1)} %fusion.58), channel_id=1, replica_groups=mesh['seq'=8,'tp'=4] {'seq'}, use_global_device_ids=true, to_apply=%region_20.21 | all-reduce | flops 8320 | bytes 66560 | tf_op jit(solution)/shard_map/psum | solution.py:119
  363.2 10.1 %psum.140 = f32[16,256]{1,0:T(8,128)S(1)} all-reduce(f32[16,256]{1,0:T(8,128)S(1)} %fusion.26), channel_id=1, replica_groups=mesh['seq'=8,'tp'=4] {'tp'}, use_global_device_ids=true, to_apply=%region_23.24 | all-reduce | flops 4096 | bytes 32768 | tf_op jit(solution)/shard_map/psum | solution.py:77
  373.4 3.6 collective-permute-done.6
  377.0 3.7 collective-permute-done.7
  380.9 4.8 collective-permute-done.8
  389.0 70.1 %all-reduce.9.cloned.1.call-done = (f32[16,2048]{1,0:T(8,128)}, f32[16,2048]{1,0:T(8,128)}) async-done(((f32[16,2048]{1,0:T(8,128)}, f32[16,2048]{1,0:T(8,128)}), (f32[16,2048]{1,0:T(8,128)}, f32[16,2048]{1,0:T(8,128)})) %all-reduce.9.cloned.1.call-update) | async-done | bytes 262160 | tf_op jit(solution)/shard_map/psum | solution.py:129
  460.7 10.1 %psum.143 = f32[16,256]{1,0:T(8,128)S(1)} all-reduce(f32[16,256]{1,0:T(8,128)S(1)} %fusion.2), channel_id=1, replica_groups=mesh['seq'=8,'tp'=4] {'tp'}, use_global_device_ids=true, to_apply=%region_27.28 | all-reduce | flops 4096 | bytes 32768 | tf_op jit(solution)/shard_map/psum | solution.py:77
  471.6 2.9 collective-permute-done.9
  475.5 2.7 collective-permute-done.10
  (125 shorter events, 45.7 us)
Async XLA Ops:
  7.2 215.4 %all-reduce.11.cloned.1.call-start = ((), (), s32[]{:S(2)}) async-start(), calls=%async_computation.1 | async-start | bytes 524288 | tf_op jit(solution)/shard_map/psum | solution.py:129
  55.5 93.7 %copy-start = (bf16[2,256,2048]{2,1,0:T(8,128)(2,1)S(1)}, bf16[2,256,2048]{2,1,0:T(8,128)(2,1)}, u32[]{:S(2)}) copy-start(bf16[2,256,2048]{2,1,0:T(8,128)(2,1)} %param.20) | copy-start | bytes 6291460
  55.7 94.5 %copy-start.10 = (pred[16,64]{1,0:T(8,128)(4,1)}, pred[16,64]{1,0:T(8,128)(4,1)S(1)}, u32[]{:S(2)}) copy-start(pred[16,64]{1,0:T(8,128)(4,1)S(1)} %get-tuple-element.40) | copy-start | bytes 3076
  55.7 94.5 %copy-start.13 = (pred[16,64]{1,0:T(8,128)(4,1)}, pred[16,64]{1,0:T(8,128)(4,1)S(1)}, u32[]{:S(2)}) copy-start(pred[16,64]{1,0:T(8,128)(4,1)S(1)} %get-tuple-element.41) | copy-start | bytes 3076
  136.8 3.7 collective-permute-start
  140.5 3.7 collective-permute-start.1
  144.2 4.9 collective-permute-start.2
  150.2 137.9 %copy-start.1 = (bf16[2,16,64,128]{3,2,1,0:T(8,128)(2,1)S(1)}, bf16[2,16,64,128]{3,2,1,0:T(8,128)(2,1)}, u32[]{:S(2)}) copy-start(bf16[2,16,64,128]{3,2,1,0:T(8,128)(2,1)} %param.23) | copy-start | bytes 1572868
  150.2 137.9 %copy-start.2 = (bf16[2,16,64,128]{3,2,1,0:T(8,128)(2,1)S(1)}, bf16[2,16,64,128]{3,2,1,0:T(8,128)(2,1)}, u32[]{:S(2)}) copy-start(bf16[2,16,64,128]{3,2,1,0:T(8,128)(2,1)} %param.22) | copy-start | bytes 1572868
  152.5 306.5 %all-reduce.9.cloned.1.call-start = ((), (), s32[]{:S(2)}) async-start(), calls=%async_computation | async-start | bytes 524288 | tf_op jit(solution)/shard_map/psum | solution.py:129
  234.3 3.7 collective-permute-start.3
  238.0 3.7 collective-permute-start.4
  241.8 4.9 collective-permute-start.5
  291.3 71.8 %copy-start.8 = (bf16[2,512,256]{2,1,0:T(8,128)(2,1)S(1)}, bf16[2,512,256]{2,1,0:T(8,128)(2,1)}, u32[]{:S(2)}) copy-start(bf16[2,512,256]{2,1,0:T(8,128)(2,1)} %param.18) | copy-start | bytes 1572868
  373.3 3.7 collective-permute-start.6
  377.0 3.7 collective-permute-start.7
  380.8 4.9 collective-permute-start.8
  385.8 94.3 %copy-start.3 = (bf16[1,16,64,128]{3,2,1,0:T(8,128)(2,1)S(1)}, bf16[1,16,64,128]{3,2,1,0:T(8,128)(2,1)}, u32[]{:S(2)}) copy-start(bf16[1,16,64,128]{3,2,1,0:T(8,128)(2,1)} %get-tuple-element.23) | copy-start | bytes 786436
  385.8 94.3 %copy-start.4 = (bf16[1,16,64,128]{3,2,1,0:T(8,128)(2,1)S(1)}, bf16[1,16,64,128]{3,2,1,0:T(8,128)(2,1)}, u32[]{:S(2)}) copy-start(bf16[1,16,64,128]{3,2,1,0:T(8,128)(2,1)} %get-tuple-element.24) | copy-start | bytes 786436
  385.9 94.3 %copy-start.5 = (bf16[1,16,64,128]{3,2,1,0:T(8,128)(2,1)S(1)}, bf16[1,16,64,128]{3,2,1,0:T(8,128)(2,1)}, u32[]{:S(2)}) copy-start(bf16[1,16,64,128]{3,2,1,0:T(8,128)(2,1)} %get-tuple-element.38) | copy-start | bytes 786436
  385.9 94.3 %copy-start.6 = (bf16[1,16,64,128]{3,2,1,0:T(8,128)(2,1)S(1)}, bf16[1,16,64,128]{3,2,1,0:T(8,128)(2,1)}, u32[]{:S(2)}) copy-start(bf16[1,16,64,128]{3,2,1,0:T(8,128)(2,1)} %get-tuple-element.39) | copy-start | bytes 786436
  470.8 3.7 collective-permute-start.9
  474.5 3.7 collective-permute-start.10
  478.3 4.9 collective-permute-start.11
  (7 other events, 217.5 us)
Sparse Core Ops, SparseCore 0:
  152.7 69.8 all-reduce.10
  389.1 69.8 all-reduce.8
